TPU v7x, 32 devices: a whole 2x2x4 slice. The times are simulated.
32 devices in a mesh: rows: 8 (over z, y), sub: 4 (over x, core).
Axes of the slice: x: 2, y: 2, z: 4, core: 2. Of those that a mesh axis runs over, the one named last changes fastest.
Arguments:
- stiffness_tiles: bfloat16 [8, 4, 128, 128, 128], P('rows', 'sub'), may hold values from -0.5 to 0.5
- damping_tiles: bfloat16 [8, 4, 128, 128, 128], P('rows', 'sub'), may hold values from -0.5 to 0.5
- tile_map: int32 [8, 4, 2, 128], P('rows', 'sub'), may hold values from -1 to 767, as said below
- inv_mass: float32 [262144], P(('rows', 'sub')), may hold values from 0.5 to 2
- spectral_shift: float32 [], replicated, may hold values from 0.5 to 1.5
- basis: float32 [58, 262144], P(None, ('rows', 'sub')), may hold values from -20 to 20
- compact: float32 [2, 58, 57], replicated, may hold values from -0.54 to 0.54
Outputs:
- new_basis: float32 [2, 262144], P(None, ('rows', 'sub'))
- compact_out: float32 [2, 60, 59], replicated
- hessenberg: float32 [59, 2], replicated
Inputs may be any that keep to these rules, and one draw needn't show every extreme that they name: tile_map[r, s, 0, t] is the tile row of part r that slot t adds to, or -1 for an unused slot; the used slots of a device come first, and some device uses all 128. tile_map[r, s, 1, t] is the source column tile counted from the start of part r - 1.
All inputs are finite; a program needn't handle non-finite values.
Results may differ from a plain program's by a relative error of at most 0.0033.
Values may be sent and summed in bfloat16 or wider, within the bound.
No kernel may reach another device: no remote copies, remote signals or barrier semaphores. Data moves between devices by JAX's collectives and lax.ppermute only.
A program may use at most 64 MiB of HBM per device.

v0:
```python
import jax
import jax.numpy as jnp
from jax import lax
from jax.sharding import PartitionSpec as P

ITERS = 2
precise = lax.Precision.HIGHEST


def padded(array, sides, width):
    for axis, dim in sides:
        devices, length = (lax.axis_size(axis), array.shape[dim])
        up = [(i, (i + 1) % devices) for i in range(devices - 1)]
        down = [(j, i) for i, j in up]
        last = lax.slice_in_dim(array, length - width, length, axis=dim)
        initial = lax.slice_in_dim(array, 0, width, axis=dim)
        before = lax.ppermute(last, axis, up)
        after = lax.ppermute(initial, axis, down)
        array = jnp.concatenate([before, array, after], axis=dim)
    return array


def compact_update(upper_half, lower_half, coefficients, norm_value, lower_tail):
    columns = upper_half.shape[1]
    zero_row = jnp.zeros((1, columns), upper_half.dtype)
    upper_ext = jnp.concatenate([upper_half, zero_row], 0)
    lower_ext = jnp.concatenate([lower_half, zero_row], 0)
    upper_coeffs = jnp.concatenate([coefficients, norm_value[None]])
    lower_coeffs = jnp.concatenate([lower_tail, jnp.zeros((1,), lower_tail.dtype)])
    weights = jnp.zeros((columns,), upper_half.dtype)
    for repeat_index in range(2):
        projection = jnp.dot(upper_coeffs, upper_ext, precision=precise) + jnp.dot(
            lower_coeffs, lower_ext, precision=precise
        )
        upper_coeffs = upper_coeffs - jnp.dot(upper_ext, projection, precision=precise)
        lower_coeffs = lower_coeffs - jnp.dot(lower_ext, projection, precision=precise)
        weights = weights + projection
    beta_norm = jnp.sqrt(
        jnp.sum(upper_coeffs * upper_coeffs) + jnp.sum(lower_coeffs * lower_coeffs) + 1e-06
    )
    upper_new = jnp.concatenate([upper_ext, (upper_coeffs / beta_norm)[:, None]], 1)
    lower_new = jnp.concatenate([lower_ext, (lower_coeffs / beta_norm)[:, None]], 1)
    return (upper_new, lower_new, weights, beta_norm)


def tile_products(damping, stiffness, target, source, blocked, tile_rows):
    picked_damp = blocked[0][source]
    picked_stiff = blocked[1][source]
    product = jnp.einsum("sij,sj->si", damping, picked_damp, preferred_element_type=jnp.float32)
    product = product + jnp.einsum(
        "sij,sj->si", stiffness, picked_stiff, preferred_element_type=jnp.float32
    )
    selector = (target[None, :] == jnp.arange(tile_rows, dtype=jnp.int32)[:, None]).astype(
        jnp.float32
    )
    return jnp.dot(selector, product, precision=precise)


def on_device(stiffness_tiles, damping_tiles, tile_map, inv_mass, spectral_shift, basis, compact):
    rows_count = lax.axis_size("rows")
    sub_count = lax.axis_size("sub")
    tile_size = stiffness_tiles.shape[-1]
    local_rows = basis.shape[1]
    part_rows = sub_count * local_rows
    tile_rows = part_rows // tile_size
    unknowns = local_rows * rows_count * sub_count
    target = tile_map[0, 0, 0]
    source = tile_map[0, 0, 1]
    damping = damping_tiles[0, 0]
    stiffness = stiffness_tiles[0, 0]
    held = basis
    upper_half = compact[0]
    lower_half = compact[1]
    new_columns = []
    hess_columns = []
    for iteration in range(ITERS):
        upper_last = upper_half[:, -1]
        lower_last = lower_half[:, -1]
        upper_vec = jnp.dot(upper_last, held, precision=precise)
        lower_vec = jnp.dot(lower_last, held, precision=precise)
        vectors = jnp.stack([upper_vec, lower_vec]).astype(jnp.bfloat16)
        whole_part = lax.all_gather(vectors, "sub", axis=1, tiled=True)
        window = padded(whole_part, (("rows", 1),), part_rows)
        blocked = window.reshape(2, 3 * tile_rows, tile_size)
        summed = tile_products(damping, stiffness, target, source, blocked, tile_rows)
        partial_value = summed.reshape(-1)
        coupled = lax.psum_scatter(partial_value, "sub", scatter_dimension=0, tiled=True)
        image = spectral_shift * upper_vec - inv_mass * coupled
        image_inner, image_self, gram = lax.psum(
            (
                jnp.dot(held, image, precision=precise),
                jnp.sum(image * image),
                jnp.dot(held, held.T, precision=precise),
            ),
            ("rows", "sub"),
        )
        first_part = image_inner / unknowns
        gram = gram / unknowns
        second_part = first_part - jnp.dot(gram, first_part, precision=precise)
        coefficients = first_part + second_part
        residual_two = image - jnp.dot(coefficients, held, precision=precise)
        square_mean = (
            image_self / unknowns
            - 2.0 * jnp.dot(coefficients, first_part, precision=precise)
            + jnp.dot(
                coefficients, jnp.dot(gram, coefficients, precision=precise), precision=precise
            )
        )
        norm_value = jnp.sqrt(square_mean + 1e-06)
        column = residual_two / norm_value
        lower_tail = upper_last + spectral_shift * lower_last
        upper_half, lower_half, weights, beta_norm = compact_update(
            upper_half, lower_half, coefficients, norm_value, lower_tail
        )
        held = jnp.concatenate([held, column[None]], 0)
        new_columns.append(column)
        hess_columns.append(
            jnp.concatenate(
                [weights, beta_norm[None], jnp.zeros((ITERS - 1 - iteration,), weights.dtype)]
            )
        )
    return (
        jnp.stack(new_columns),
        jnp.stack([upper_half, lower_half]),
        jnp.stack(hess_columns, axis=1),
    )


def solution(mesh):
    in_specs = (
        P("rows", "sub", None, None, None),
        P("rows", "sub", None, None, None),
        P("rows", "sub", None, None),
        P(("rows", "sub")),
        P(),
        P(None, ("rows", "sub")),
        P(),
    )
    out_specs = (P(None, ("rows", "sub")), P(), P())
    return jax.shard_map(
        on_device, mesh=mesh, in_specs=in_specs, out_specs=out_specs, check_vma=False
    )
```

profile of v0, /device:TPU:0, one launch (start us, length us, event | category | flops | bytes accessed | tf_op | source)
XLA Modules:
  0.0 251.9 jit_solution(1315669255677280857)
XLA Ops:
  8.7 2.7 %fusion.54 = f32[1,8192]{1,0:T(1,128)S(1)} fusion(f32[58,8192]{1,0:T(8,128)} %param.12, f32[58]{0:T(128)S(1)} %get-tuple-element.48), kind=kOutput, calls=%fused_computation.120 | convolution fusion | flops 5701632 | bytes 1933544 | tf_op jit(solution)/shard_map/dot_general | solution.py:79
  12.6 6.5 %all_gather.6 = bf16[2,32768]{1,0:T(2,128)(2,1)S(1)} all-gather(bf16[2,8192]{1,0:T(2,128)(2,1)S(1)} %pad_maximum_fusion.8), channel_id=1, replica_groups=mesh['rows'=8,'sub'=4] {'sub'}, dimensions={1}, use_global_device_ids=true | all-gather | bytes 163840 | tf_op jit(solution)/shard_map/all_gather | solution.py:82
  19.1 3.9 %collective-permute-start = (bf16[2,32768]{1,0:T(2,128)(2,1)S(1)}, bf16[2,32768]{1,0:T(2,128)(2,1)S(1)}, u32[]{:S(2)}, u32[]{:S(2)}) collective-permute-start(bf16[2,32768]{1,0:T(2,128)(2,1)S(1)} %all_gather.6), channel_id=1, source_target_pairs={{0,4},{4,8},{8,12},{12,16},{16,20},{20,24},{24,28},{1,5},{5,9},{9,... | collective-permute-start | bytes 393224 | tf_op jit(solution)/shard_map/ppermute | solution.py:17
  23.1 1.3 collective-permute-start.1
  24.4 1.8 fusion.115
  27.1 3.4 %collective-permute-done.1 = bf16[2,32768]{1,0:T(2,128)(2,1)S(1)} collective-permute-done((bf16[2,32768]{1,0:T(2,128)(2,1)S(1)}, bf16[2,32768]{1,0:T(2,128)(2,1)S(1)}, u32[]{:S(2)}, u32[]{:S(2)}) %collective-permute-start.1) | collective-permute-done | bytes 131104 | tf_op jit(solution)/shard_map/ppermute | solution.py:18
  30.5 2.1 slice_reduce_fusion.2
  34.0 4.6 %fusion.6 = f32[128,1,128]{2,1,0:T(1,128)S(1)} fusion(bf16[1,1,128,128,128]{4,3,2,1,0:T(8,128)(2,1)} %param.8, bf16[128,128,1]{1,0,2:T(8,128)(2,1)S(1)} %bitcast.283), kind=kOutput, calls=%fused_computation.12 | convolution fusion | flops 4194304 | bytes 4292608 | tf_op jit(solution)/shard_map/sij,sj->si/dot_general | solution.py:49
  38.6 2.3 fusion.2
  43.2 31.7 %all-reduce.11.cloned.1.call-done = f32[32768]{0:T(1024)} async-done(((f32[32768]{0:T(1024)}), f32[32768]{0:T(1024)}) %all-reduce.11.cloned.1.call-update) | async-done | bytes 131088
  74.9 1.4 multiply_reduce_fusion.1
  76.3 1.7 convolution_bitcast_fusion.23
  78.0 39.9 %all-reduce.7 = (f32[58,58]{1,0:T(8,128)S(1)}, f32[58]{0:T(128)S(1)}, f32[]{:T(128)}) all-reduce(f32[58,58]{1,0:T(8,128)S(1)} %fusion.115, f32[58]{0:T(128)S(1)} %convolution_bitcast_fusion.23, f32[]{:T(128)} %get-tuple-element.27), channel_id=1, replica_groups=mesh['rows'=8,'sub'=4] {'rows','sub'}, use_global_device_ids=true, to_apply=%region_2.0 | all-reduce | flops 3423 | bytes 27384 | tf_op jit(solution)/shard_map/psum | solution.py:89
  129.0 5.8 %all_gather.7 = bf16[2,32768]{1,0:T(2,128)(2,1)S(1)} all-gather(bf16[2,8192]{1,0:T(2,128)(2,1)S(1)} %pad_maximum_fusion.9), channel_id=1, replica_groups=mesh['rows'=8,'sub'=4] {'sub'}, dimensions={1}, use_global_device_ids=true | all-gather | bytes 163840 | tf_op jit(solution)/shard_map/all_gather | solution.py:82
  134.8 3.8 %collective-permute-start.2 = (bf16[2,32768]{1,0:T(2,128)(2,1)S(1)}, bf16[2,32768]{1,0:T(2,128)(2,1)S(1)}, u32[]{:S(2)}, u32[]{:S(2)}) collective-permute-start(bf16[2,32768]{1,0:T(2,128)(2,1)S(1)} %all_gather.7), channel_id=1, source_target_pairs={{0,4},{4,8},{8,12},{12,16},{16,20},{20,24},{24,28},{1,5},{5,9},{9,... | collective-permute-start | bytes 393224 | tf_op jit(solution)/shard_map/ppermute | solution.py:17
  139.9 1.8 fusion.29
  142.3 3.7 %collective-permute-done.3 = bf16[2,32768]{1,0:T(2,128)(2,1)S(1)} collective-permute-done((bf16[2,32768]{1,0:T(2,128)(2,1)S(1)}, bf16[2,32768]{1,0:T(2,128)(2,1)S(1)}, u32[]{:S(2)}, u32[]{:S(2)}) %collective-permute-start.3) | collective-permute-done | bytes 131104 | tf_op jit(solution)/shard_map/ppermute | solution.py:18
  146.0 2.1 slice_reduce_fusion
  148.8 4.4 %fusion = f32[128,1,128]{2,1,0:T(1,128)S(1)} fusion(bf16[1,1,128,128,128]{4,3,2,1,0:T(8,128)(2,1)} %param.7, bf16[128,128,1]{1,0,2:T(8,128)(2,1)S(1)} %bitcast.286), kind=kOutput, calls=%fused_computation.6 | convolution fusion | flops 4194304 | bytes 4292608 | tf_op jit(solution)/shard_map/sij,sj->si/dot_general | solution.py:50
  154.0 4.4 %fusion.4 = f32[128,1,128]{2,1,0:T(1,128)S(1)} fusion(bf16[1,1,128,128,128]{4,3,2,1,0:T(8,128)(2,1)} %param.8, bf16[128,128,1]{1,0,2:T(8,128)(2,1)S(1)} %bitcast.285), kind=kOutput, calls=%fused_computation.10 | convolution fusion | flops 4194304 | bytes 4292608 | tf_op jit(solution)/shard_map/sij,sj->si/dot_general | solution.py:49
  159.4 31.7 %all-reduce.13.cloned.1.call-done = f32[32768]{0:T(1024)} async-done(((f32[32768]{0:T(1024)}), f32[32768]{0:T(1024)}) %all-reduce.13.cloned.1.call-update) | async-done | bytes 131088
  191.1 1.4 multiply_reduce_fusion
  192.5 1.7 convolution_bitcast_fusion.22
  194.2 39.7 %all-reduce.6 = (f32[59,59]{1,0:T(8,128)S(1)}, f32[59]{0:T(128)S(1)}, f32[]{:T(128)}) all-reduce(f32[59,59]{1,0:T(8,128)S(1)} %fusion.29, f32[59]{0:T(128)S(1)} %convolution_bitcast_fusion.22, f32[]{:T(128)} %get-tuple-element.25), channel_id=1, replica_groups=mesh['rows'=8,'sub'=4] {'rows','sub'}, use_global_device_ids=true, to_apply=%region_9.0 | all-reduce | flops 3541 | bytes 28328 | tf_op jit(solution)/shard_map/psum | solution.py:89
  (94 shorter events, 25.9 us)
Async XLA Ops:
  7.2 4.2 %copy-start = (f32[58,8192]{1,0:T(8,128)S(1)}, f32[58,8192]{1,0:T(8,128)}, u32[]{:S(2)}) copy-start(f32[58,8192]{1,0:T(8,128)} %param.12) | copy-start | bytes 5701636
  7.2 67.7 %all-reduce.11.cloned.1.call-start = ((), (), s32[]{:S(2)}) async-start(), calls=%async_computation | async-start | bytes 262144
  19.1 7.0 %copy-start.3 = (s32[1,1,2,128]{3,2,1,0:T(2,128)S(1)}, s32[1,1,2,128]{3,2,1,0:T(2,128)}, u32[]{:S(2)}) copy-start(s32[1,1,2,128]{3,2,1,0:T(2,128)} %param.9) | copy-start | bytes 3076
  19.1 7.7 %collective-permute-start = (bf16[2,32768]{1,0:T(2,128)(2,1)S(1)}, bf16[2,32768]{1,0:T(2,128)(2,1)S(1)}, u32[]{:S(2)}, u32[]{:S(2)}) collective-permute-start(bf16[2,32768]{1,0:T(2,128)(2,1)S(1)} %all_gather.6), channel_id=1, source_target_pairs={{0,4},{4,8},{8,12},{12,16},{16,20},{20,24},{24,28},{1,5},{5,9},{9,... | collective-permute-start | bytes 393224 | tf_op jit(solution)/shard_map/ppermute | solution.py:17
  23.1 7.4 %collective-permute-start.1 = (bf16[2,32768]{1,0:T(2,128)(2,1)S(1)}, bf16[2,32768]{1,0:T(2,128)(2,1)S(1)}, u32[]{:S(2)}, u32[]{:S(2)}) collective-permute-start(bf16[2,32768]{1,0:T(2,128)(2,1)S(1)} %all_gather.6), channel_id=1, source_target_pairs={{4,0},{8,4},{12,8},{16,12},{20,16},{24,20},{28,24},{5,1},{9,5},{13... | collective-permute-start | bytes 393224 | tf_op jit(solution)/shard_map/ppermute | solution.py:18
  34.0 4.6 %copy-start.1 = (bf16[1,1,128,128,128]{4,3,2,1,0:T(8,128)(2,1)S(1)}, bf16[1,1,128,128,128]{4,3,2,1,0:T(8,128)(2,1)}, u32[]{:S(2)}) copy-start(bf16[1,1,128,128,128]{4,3,2,1,0:T(8,128)(2,1)} %param.7) | copy-start | bytes 12582916
  38.6 3.3 %copy-start.4 = (u32[32]{0:T(128)S(1)}, u32[32]{0:T(128)}, u32[]{:S(2)}) copy-start(u32[32]{0:T(128)} %constant.43) | copy-start | bytes 388
  38.6 36.3 %copy-start.2 = (f32[8192]{0:T(1024)S(1)}, f32[8192]{0:T(1024)}, u32[]{:S(2)}) copy-start(f32[8192]{0:T(1024)} %param.10) | copy-start | bytes 98308
  41.8 149.3 %all-reduce.13.cloned.1.call-start = ((), (), s32[]{:S(2)}) async-start(), calls=%async_computation.1 | async-start | bytes 262144
  134.8 7.2 %collective-permute-start.2 = (bf16[2,32768]{1,0:T(2,128)(2,1)S(1)}, bf16[2,32768]{1,0:T(2,128)(2,1)S(1)}, u32[]{:S(2)}, u32[]{:S(2)}) collective-permute-start(bf16[2,32768]{1,0:T(2,128)(2,1)S(1)} %all_gather.7), channel_id=1, source_target_pairs={{0,4},{4,8},{8,12},{12,16},{16,20},{20,24},{24,28},{1,5},{5,9},{9,... | collective-permute-start | bytes 393224 | tf_op jit(solution)/shard_map/ppermute | solution.py:17
  138.6 7.4 %collective-permute-start.3 = (bf16[2,32768]{1,0:T(2,128)(2,1)S(1)}, bf16[2,32768]{1,0:T(2,128)(2,1)S(1)}, u32[]{:S(2)}, u32[]{:S(2)}) collective-permute-start(bf16[2,32768]{1,0:T(2,128)(2,1)S(1)} %all_gather.7), channel_id=1, source_target_pairs={{4,0},{8,4},{12,8},{16,12},{20,16},{24,20},{28,24},{5,1},{9,5},{13... | collective-permute-start | bytes 393224 | tf_op jit(solution)/shard_map/ppermute | solution.py:18
Sparse Core Ops, SparseCore 0:
  41.9 32.9 all-reduce.10
  159.5 31.5 all-reduce.12
where the time goes:
time: 253 us; the launch traced here: 252 us
  blocking collectives  91.9 us (36%)
  waiting for transfers between devices  70.5 us (28%)
  matrix products  41.1 us (16%)
  between operations  22.3 us (9%)
  local copies, waits for them, and re-layouts  10.9 us (4%)
  starting transfers between devices  10.4 us (4%)
  other arithmetic  4.73 us (2%)
    psum x2, blocking collectives, on_device(): lax.psum((jnp.dot(held, image, precision=precise), jnp.sum(image * image)...  79.6 us
    unnamed x4, waiting for transfers between devices  63.4 us
    all_gather x2, blocking collectives, on_device(): whole_part = lax.all_gather(vectors, 'sub', axis=1, tiled=True)  12.3 us
    dot_general x2, matrix products, tile_products(): jnp.einsum('sij,sj->si', damping, picked_damp, preferred_element_type=jnp...  9.01 us
    ppermute x2, starting transfers between devices, padded(): before = lax.ppermute(last, axis, up)  7.71 us
    ppermute x2, waiting for transfers between devices, padded(): after = lax.ppermute(initial, axis, down)  7.03 us
    dot_general x2, matrix products, tile_products(): jnp.einsum('sij,sj->si', stiffness, picked_stiff, preferred_element_type=...  6.71 us
  transfers between devices with their start and end apart: 6, of which 4 were waited for; matrix products, arithmetic and copies ran while one was open for 2% of the time, Pallas kernels for 0%

commit v1 on v0

--- a/solution.py
+++ b/solution.py
@@ -87,12 +87,15 @@
         coupled = lax.psum_scatter(partial_value, "sub", scatter_dimension=0, tiled=True)
         image = spectral_shift * upper_vec - inv_mass * coupled
         image_inner, image_self, gram = lax.psum(
-            (
-                jnp.dot(held, image, precision=precise),
-                jnp.sum(image * image),
-                jnp.dot(held, held.T, precision=precise),
+            lax.psum(
+                (
+                    jnp.dot(held, image, precision=precise),
+                    jnp.sum(image * image),
+                    jnp.dot(held, held.T, precision=precise),
+                ),
+                "sub",
             ),
-            ("rows", "sub"),
+            "rows",
         )
         first_part = image_inner / unknowns
         gram = gram / unknowns

time: 253 us -> 269 us (1.063)
  blocking collectives: 91.9 us -> 112 us
    psum x0 -> x2, blocking collectives: none -> 77.1 us  [on_device(): lax.psum(lax.psum((jnp.dot(held, image, precision=precise), jnp.sum(image...]
    psum x2, blocking collectives: 79.6 us -> 23 us  [on_device(): lax.psum((jnp.dot(held, image, precision=precise), jnp.sum(image * image)...]
  transfers between devices with their start and end apart: 6 -> 6, of which waited for: 4 -> 5; matrix products, arithmetic and copies ran while one was open for 2% -> 2% of each run, Pallas kernels for 0% -> 0%
where the time goes in v1:
time: 269 us; the launch traced here: 268 us
  blocking collectives  112 us (42%)
  waiting for transfers between devices  69.5 us (26%)
  matrix products  41.1 us (15%)
  between operations  22.3 us (8%)
  local copies, waits for them, and re-layouts  10.9 us (4%)
  starting transfers between devices  7.88 us (3%)
  other arithmetic  4.73 us (2%)
    psum x2, blocking collectives, on_device(): lax.psum(lax.psum((jnp.dot(held, image, precision=precise), jnp.sum(image...  77.1 us
    unnamed x4, waiting for transfers between devices  62.1 us
    psum x2, blocking collectives, on_device(): lax.psum((jnp.dot(held, image, precision=precise), jnp.sum(image * image)...  23 us
    all_gather x2, blocking collectives, on_device(): whole_part = lax.all_gather(vectors, 'sub', axis=1, tiled=True)  11.9 us
    dot_general x2, matrix products, tile_products(): jnp.einsum('sij,sj->si', damping, picked_damp, preferred_element_type=jnp...  9.02 us
    ppermute x2, waiting for transfers between devices, padded(): after = lax.ppermute(initial, axis, down)  7.23 us
    dot_general x2, matrix products, tile_products(): jnp.einsum('sij,sj->si', stiffness, picked_stiff, preferred_element_type=...  6.71 us
  transfers between devices with their start and end apart: 6, of which 5 were waited for; matrix products, arithmetic and copies ran while one was open for 2% of the time, Pallas kernels for 0%

profile of v1, /device:TPU:0, one launch (start us, length us, event | category | flops | bytes accessed | tf_op | source)
XLA Modules:
  0.0 268.5 jit_solution(12291621375483048990)
XLA Ops:
  8.7 2.7 %fusion.54 = f32[1,8192]{1,0:T(1,128)S(1)} fusion(f32[58,8192]{1,0:T(8,128)} %param.12, f32[58]{0:T(128)S(1)} %get-tuple-element.54), kind=kOutput, calls=%fused_computation.120 | convolution fusion | flops 5701632 | bytes 1933544 | tf_op jit(solution)/shard_map/dot_general | solution.py:79
  12.6 6.5 %all_gather.6 = bf16[2,32768]{1,0:T(2,128)(2,1)S(1)} all-gather(bf16[2,8192]{1,0:T(2,128)(2,1)S(1)} %pad_maximum_fusion.8), channel_id=1, replica_groups=mesh['rows'=8,'sub'=4] {'sub'}, dimensions={1}, use_global_device_ids=true | all-gather | bytes 163840 | tf_op jit(solution)/shard_map/all_gather | solution.py:82
  19.1 3.9 %collective-permute-start = (bf16[2,32768]{1,0:T(2,128)(2,1)S(1)}, bf16[2,32768]{1,0:T(2,128)(2,1)S(1)}, u32[]{:S(2)}, u32[]{:S(2)}) collective-permute-start(bf16[2,32768]{1,0:T(2,128)(2,1)S(1)} %all_gather.6), channel_id=1, source_target_pairs={{0,4},{4,8},{8,12},{12,16},{16,20},{20,24},{24,28},{1,5},{5,9},{9,... | collective-permute-start | bytes 393224 | tf_op jit(solution)/shard_map/ppermute | solution.py:17
  24.4 1.8 fusion.115
  27.1 3.4 %collective-permute-done.1 = bf16[2,32768]{1,0:T(2,128)(2,1)S(1)} collective-permute-done((bf16[2,32768]{1,0:T(2,128)(2,1)S(1)}, bf16[2,32768]{1,0:T(2,128)(2,1)S(1)}, u32[]{:S(2)}, u32[]{:S(2)}) %collective-permute-start.1) | collective-permute-done | bytes 131104 | tf_op jit(solution)/shard_map/ppermute | solution.py:18
  30.5 2.1 slice_reduce_fusion.2
  34.0 4.6 %fusion.6 = f32[128,1,128]{2,1,0:T(1,128)S(1)} fusion(bf16[1,1,128,128,128]{4,3,2,1,0:T(8,128)(2,1)} %param.8, bf16[128,128,1]{1,0,2:T(8,128)(2,1)S(1)} %bitcast.283), kind=kOutput, calls=%fused_computation.12 | convolution fusion | flops 4194304 | bytes 4292608 | tf_op jit(solution)/shard_map/sij,sj->si/dot_general | solution.py:49
  38.6 2.3 fusion.2
  43.2 31.7 %all-reduce.13.cloned.1.call-done = f32[32768]{0:T(1024)} async-done(((f32[32768]{0:T(1024)}), f32[32768]{0:T(1024)}) %all-reduce.13.cloned.1.call-update) | async-done | bytes 131088
  74.9 1.4 multiply_reduce_fusion.1
  76.3 1.7 convolution_bitcast_fusion.23
  78.0 11.5 %all-reduce.9 = (f32[58,58]{1,0:T(8,128)S(1)}, f32[58]{0:T(128)S(1)}, f32[]{:T(128)}) all-reduce(f32[58,58]{1,0:T(8,128)S(1)} %fusion.115, f32[58]{0:T(128)S(1)} %convolution_bitcast_fusion.23, f32[]{:T(128)} %get-tuple-element.33), channel_id=1, replica_groups=mesh['rows'=8,'sub'=4] {'sub'}, use_global_device_ids=true, to_apply=%region_3.0 | all-reduce | flops 3423 | bytes 27384 | tf_op jit(solution)/shard_map/psum | solution.py:90
  89.5 38.5 %all-reduce.7 = (f32[58,58]{1,0:T(8,128)S(1)}, f32[58]{0:T(128)S(1)}, f32[]{:T(128)}) all-reduce(f32[58,58]{1,0:T(8,128)S(1)} %get-tuple-element.25, f32[58]{0:T(128)S(1)} %get-tuple-element.26, f32[]{:T(128)} %get-tuple-element.27), channel_id=1, replica_groups=mesh['rows'=8,'sub'=4] {'rows'}, use_global_device_ids=true, to_apply=%region_4.0 | all-reduce | flops 3423 | bytes 27384 | tf_op jit(solution)/shard_map/psum | solution.py:89
  139.1 5.4 %all_gather.7 = bf16[2,32768]{1,0:T(2,128)(2,1)S(1)} all-gather(bf16[2,8192]{1,0:T(2,128)(2,1)S(1)} %pad_maximum_fusion.9), channel_id=1, replica_groups=mesh['rows'=8,'sub'=4] {'sub'}, dimensions={1}, use_global_device_ids=true | all-gather | bytes 163840 | tf_op jit(solution)/shard_map/all_gather | solution.py:82
  147.1 1.8 fusion.29
  149.6 3.9 %collective-permute-done.3 = bf16[2,32768]{1,0:T(2,128)(2,1)S(1)} collective-permute-done((bf16[2,32768]{1,0:T(2,128)(2,1)S(1)}, bf16[2,32768]{1,0:T(2,128)(2,1)S(1)}, u32[]{:S(2)}, u32[]{:S(2)}) %collective-permute-start.3) | collective-permute-done | bytes 131104 | tf_op jit(solution)/shard_map/ppermute | solution.py:18
  153.6 2.1 slice_reduce_fusion
  156.4 4.4 %fusion = f32[128,1,128]{2,1,0:T(1,128)S(1)} fusion(bf16[1,1,128,128,128]{4,3,2,1,0:T(8,128)(2,1)} %param.7, bf16[128,128,1]{1,0,2:T(8,128)(2,1)S(1)} %bitcast.286), kind=kOutput, calls=%fused_computation.6 | convolution fusion | flops 4194304 | bytes 4292608 | tf_op jit(solution)/shard_map/sij,sj->si/dot_general | solution.py:50
  161.5 4.4 %fusion.4 = f32[128,1,128]{2,1,0:T(1,128)S(1)} fusion(bf16[1,1,128,128,128]{4,3,2,1,0:T(8,128)(2,1)} %param.8, bf16[128,128,1]{1,0,2:T(8,128)(2,1)S(1)} %bitcast.285), kind=kOutput, calls=%fused_computation.10 | convolution fusion | flops 4194304 | bytes 4292608 | tf_op jit(solution)/shard_map/sij,sj->si/dot_general | solution.py:49
  167.0 30.4 %all-reduce.15.cloned.1.call-done = f32[32768]{0:T(1024)} async-done(((f32[32768]{0:T(1024)}), f32[32768]{0:T(1024)}) %all-reduce.15.cloned.1.call-update) | async-done | bytes 131088
  197.3 1.4 multiply_reduce_fusion
  198.7 1.7 convolution_bitcast_fusion.22
  200.4 11.5 %all-reduce.8 = (f32[59,59]{1,0:T(8,128)S(1)}, f32[59]{0:T(128)S(1)}, f32[]{:T(128)}) all-reduce(f32[59,59]{1,0:T(8,128)S(1)} %fusion.29, f32[59]{0:T(128)S(1)} %convolution_bitcast_fusion.22, f32[]{:T(128)} %get-tuple-element.31), channel_id=1, replica_groups=mesh['rows'=8,'sub'=4] {'sub'}, use_global_device_ids=true, to_apply=%region_13.0 | all-reduce | flops 3541 | bytes 28328 | tf_op jit(solution)/shard_map/psum | solution.py:90
  211.9 38.5 %all-reduce.6 = (f32[59,59]{1,0:T(8,128)S(1)}, f32[59]{0:T(128)S(1)}, f32[]{:T(128)}) all-reduce(f32[59,59]{1,0:T(8,128)S(1)} %get-tuple-element.22, f32[59]{0:T(128)S(1)} %get-tuple-element.23, f32[]{:T(128)} %get-tuple-element.24), channel_id=1, replica_groups=mesh['rows'=8,'sub'=4] {'rows'}, use_global_device_ids=true, to_apply=%region_14.0 | all-reduce | flops 3541 | bytes 28328 | tf_op jit(solution)/shard_map/psum | solution.py:89
  (96 shorter events, 28.6 us)
Async XLA Ops:
  7.2 4.2 %copy-start = (f32[58,8192]{1,0:T(8,128)S(1)}, f32[58,8192]{1,0:T(8,128)}, u32[]{:S(2)}) copy-start(f32[58,8192]{1,0:T(8,128)} %param.12) | copy-start | bytes 5701636
  7.2 67.7 %all-reduce.13.cloned.1.call-start = ((), (), s32[]{:S(2)}) async-start(), calls=%async_computation | async-start | bytes 262144
  19.1 7.0 %copy-start.3 = (s32[1,1,2,128]{3,2,1,0:T(2,128)S(1)}, s32[1,1,2,128]{3,2,1,0:T(2,128)}, u32[]{:S(2)}) copy-start(s32[1,1,2,128]{3,2,1,0:T(2,128)} %param.9) | copy-start | bytes 3076
  19.1 7.7 %collective-permute-start = (bf16[2,32768]{1,0:T(2,128)(2,1)S(1)}, bf16[2,32768]{1,0:T(2,128)(2,1)S(1)}, u32[]{:S(2)}, u32[]{:S(2)}) collective-permute-start(bf16[2,32768]{1,0:T(2,128)(2,1)S(1)} %all_gather.6), channel_id=1, source_target_pairs={{0,4},{4,8},{8,12},{12,16},{16,20},{20,24},{24,28},{1,5},{5,9},{9,... | collective-permute-start | bytes 393224 | tf_op jit(solution)/shard_map/ppermute | solution.py:17
  23.1 7.4 %collective-permute-start.1 = (bf16[2,32768]{1,0:T(2,128)(2,1)S(1)}, bf16[2,32768]{1,0:T(2,128)(2,1)S(1)}, u32[]{:S(2)}, u32[]{:S(2)}) collective-permute-start(bf16[2,32768]{1,0:T(2,128)(2,1)S(1)} %all_gather.6), channel_id=1, source_target_pairs={{4,0},{8,4},{12,8},{16,12},{20,16},{24,20},{28,24},{5,1},{9,5},{13... | collective-permute-start | bytes 393224 | tf_op jit(solution)/shard_map/ppermute | solution.py:18
  34.0 4.6 %copy-start.1 = (bf16[1,1,128,128,128]{4,3,2,1,0:T(8,128)(2,1)S(1)}, bf16[1,1,128,128,128]{4,3,2,1,0:T(8,128)(2,1)}, u32[]{:S(2)}) copy-start(bf16[1,1,128,128,128]{4,3,2,1,0:T(8,128)(2,1)} %param.7) | copy-start | bytes 12582916
  38.6 3.3 %copy-start.4 = (u32[32]{0:T(128)S(1)}, u32[32]{0:T(128)}, u32[]{:S(2)}) copy-start(u32[32]{0:T(128)} %constant.43) | copy-start | bytes 388
  38.6 36.3 %copy-start.2 = (f32[8192]{0:T(1024)S(1)}, f32[8192]{0:T(1024)}, u32[]{:S(2)}) copy-start(f32[8192]{0:T(1024)} %param.10) | copy-start | bytes 98308
  41.8 155.5 %all-reduce.15.cloned.1.call-start = ((), (), s32[]{:S(2)}) async-start(), calls=%async_computation.1 | async-start | bytes 262144
  144.5 4.9 %collective-permute-start.2 = (bf16[2,32768]{1,0:T(2,128)(2,1)S(1)}, bf16[2,32768]{1,0:T(2,128)(2,1)S(1)}, u32[]{:S(2)}, u32[]{:S(2)}) collective-permute-start(bf16[2,32768]{1,0:T(2,128)(2,1)S(1)} %all_gather.7), channel_id=1, source_target_pairs={{0,4},{4,8},{8,12},{12,16},{16,20},{20,24},{24,28},{1,5},{5,9},{9,... | collective-permute-start | bytes 393224 | tf_op jit(solution)/shard_map/ppermute | solution.py:17
  145.8 7.6 %collective-permute-start.3 = (bf16[2,32768]{1,0:T(2,128)(2,1)S(1)}, bf16[2,32768]{1,0:T(2,128)(2,1)S(1)}, u32[]{:S(2)}, u32[]{:S(2)}) collective-permute-start(bf16[2,32768]{1,0:T(2,128)(2,1)S(1)} %all_gather.7), channel_id=1, source_target_pairs={{4,0},{8,4},{12,8},{16,12},{20,16},{24,20},{28,24},{5,1},{9,5},{13... | collective-permute-start | bytes 393224 | tf_op jit(solution)/shard_map/ppermute | solution.py:18
Sparse Core Ops, SparseCore 0:
  41.9 32.9 all-reduce.12
  167.0 30.2 all-reduce.14
